TPU v7x, 32 devices: a whole 2x2x4 slice. The times are simulated.
32 devices in a mesh: dp: 4 (over x, core), tensor: 8 (over z, y).
Axes of the slice: x: 2, y: 2, z: 4, core: 2. Of those that a mesh axis runs over, the one named last changes fastest.
Arguments:
- tokens: bfloat16 [12288, 1024], P(('dp', 'tensor')), may hold values from -6 to 6
- seq_ids: int32 [12288], P('dp'), may hold values from 0 to 11, as said below
- blk_ids: int32 [12288], P('dp'), may hold values from 0 to 11, as said below
- norm1_gain: bfloat16 [1024], P('dp'), may hold values from 0.099609375 to 1.8984375
- w_query: bfloat16 [1024, 1024], P('dp', 'tensor'), may hold values from -0.375 to 0.375
- w_key: bfloat16 [1024, 1024], P('dp', 'tensor'), may hold values from -0.1875 to 0.1875
- w_value: bfloat16 [1024, 1024], P('dp', 'tensor'), may hold values from -0.1875 to 0.1875
- w_out: bfloat16 [1024, 1024], P('tensor', 'dp'), may hold values from -0.75 to 0.75
- norm2_gain: bfloat16 [1024], P('dp'), may hold values from 0.099609375 to 1.8984375
- w_gate: bfloat16 [1024, 4096], P('dp', 'tensor'), may hold values from -0.1875 to 0.1875
- w_up: bfloat16 [1024, 4096], P('dp', 'tensor'), may hold values from -0.1875 to 0.1875
- w_down: bfloat16 [4096, 1024], P('tensor', 'dp'), may hold values from -0.09375 to 0.09375
- cotangent: bfloat16 [12288, 1024], P(('dp', 'tensor')), may hold values from -6 to 6
Outputs:
- output: bfloat16 [12288, 1024], P(('dp', 'tensor'))
- input_grad: bfloat16 [12288, 1024], P(('dp', 'tensor'))
- grad_query: float32 [1024, 1024], P('dp', 'tensor')
- grad_key: float32 [1024, 1024], P('dp', 'tensor')
- grad_value: float32 [1024, 1024], P('dp', 'tensor')
- grad_out: float32 [1024, 1024], P('tensor', 'dp')
- grad_gate: float32 [1024, 4096], P('dp', 'tensor')
- grad_up: float32 [1024, 4096], P('dp', 'tensor')
- grad_down: float32 [4096, 1024], P('tensor', 'dp')
- grad_norm1: float32 [1024], P(('dp', 'tensor'))
- grad_norm2: float32 [1024], P(('dp', 'tensor'))
Inputs may be any that keep to these rules, and one draw needn't show every extreme that they name: `seq_ids`: sequence ids never fall along the tokens; each sequence is a whole number of aligned runs of 1024 tokens and lies within one aligned run of 3072 tokens. `blk_ids`: the block index of a token is its position within its sequence divided by 256, rounded down.
All inputs are finite; a program needn't handle non-finite values.
Results may differ from a plain program's by a relative error of at most 0.02.
Values may be sent and summed in bfloat16 or wider, within the bound.
No kernel may reach another device: no remote copies, remote signals or barrier semaphores. Data moves between devices by JAX's collectives and lax.ppermute only.
A program may use at most 128 MiB of HBM per device.

v0:
```python
import jax
import jax.numpy as jnp
from jax import lax
from jax.sharding import PartitionSpec as P

DH = 64
EPS = 1e-06
NEG = -1e30


def row_scale(values):
    return lax.rsqrt(jnp.mean(values * values, axis=-1, keepdims=True) + EPS)


def norm_back(grad_normed, values, scale, gain):
    weighted = grad_normed * gain
    inner = jnp.mean(weighted * values, axis=-1, keepdims=True)
    grad_values = scale * weighted - values * (scale * scale * scale) * inner
    grad_gain = jnp.sum(grad_normed * values * scale, axis=0)
    return (grad_values, grad_gain)


def allowed_mask(seq_ids, blk_ids, start, count):
    query_seq = lax.dynamic_slice_in_dim(seq_ids, start, count, 0)
    query_blk = lax.dynamic_slice_in_dim(blk_ids, start, count, 0)
    return (query_seq[:, None] == seq_ids[None, :]) & (blk_ids[None, :] <= query_blk[:, None])


def attention_forward(queries, keys, values, seq_ids, blk_ids, factor):
    rows, heads, width = queries.shape
    block = min(512, rows)

    def one_block(start):
        query_block = lax.dynamic_slice_in_dim(queries, start, block, 0)
        allowed = allowed_mask(seq_ids, blk_ids, start, block)
        scores = (
            jnp.einsum("qhd,khd->hqk", query_block, keys, preferred_element_type=jnp.float32)
            * factor
        )
        scores = jnp.where(allowed[None], scores, NEG)
        highest = jnp.max(scores, axis=-1, keepdims=True)
        weights = jnp.exp(scores - highest)
        totals = jnp.sum(weights, axis=-1, keepdims=True)
        probs = (weights / totals).astype(jnp.bfloat16)
        mixed = jnp.einsum("hqk,khd->qhd", probs, values, preferred_element_type=jnp.float32)
        return (mixed.astype(jnp.bfloat16), (highest + jnp.log(totals))[..., 0])

    starts = jnp.arange(rows // block, dtype=jnp.int32) * block
    mixed, logsum = lax.map(one_block, starts)
    return (mixed.reshape(rows, heads * width), logsum)


def attention_backward(queries, keys, values, grad_mixed, logsum, seq_ids, blk_ids, factor):
    rows, heads, width = queries.shape
    block = min(512, rows)
    grad_heads = grad_mixed.reshape(rows, heads, width)

    def one_block(carry, inputs):
        start, block_logsum = inputs
        grad_keys, grad_values = carry
        query_block = lax.dynamic_slice_in_dim(queries, start, block, 0)
        grad_block = lax.dynamic_slice_in_dim(grad_heads, start, block, 0)
        allowed = allowed_mask(seq_ids, blk_ids, start, block)
        scores = (
            jnp.einsum("qhd,khd->hqk", query_block, keys, preferred_element_type=jnp.float32)
            * factor
        )
        scores = jnp.where(allowed[None], scores, NEG)
        probs = jnp.exp(scores - block_logsum[..., None])
        grad_probs = jnp.einsum(
            "qhd,khd->hqk", grad_block, values, preferred_element_type=jnp.float32
        )
        inner = jnp.sum(probs * grad_probs, axis=-1, keepdims=True)
        grad_scores = (probs * (grad_probs - inner)).astype(jnp.bfloat16)
        grad_query = (
            jnp.einsum("hqk,khd->qhd", grad_scores, keys, preferred_element_type=jnp.float32)
            * factor
        )
        grad_keys = (
            grad_keys
            + jnp.einsum(
                "hqk,qhd->khd", grad_scores, query_block, preferred_element_type=jnp.float32
            )
            * factor
        )
        grad_values = grad_values + jnp.einsum(
            "hqk,qhd->khd",
            probs.astype(jnp.bfloat16),
            grad_block,
            preferred_element_type=jnp.float32,
        )
        return ((grad_keys, grad_values), grad_query.astype(jnp.bfloat16))

    starts = jnp.arange(rows // block, dtype=jnp.int32) * block
    zeros = jnp.zeros((rows, heads, width), jnp.float32)
    (grad_keys, grad_values), grad_queries = lax.scan(one_block, (zeros, zeros), (starts, logsum))
    return (
        grad_queries.reshape(rows, heads * width),
        grad_keys.astype(jnp.bfloat16).reshape(rows, heads * width),
        grad_values.astype(jnp.bfloat16).reshape(rows, heads * width),
    )


def on_device(
    tokens,
    seq_ids,
    blk_ids,
    norm1_gain,
    w_query,
    w_key,
    w_value,
    w_out,
    norm2_gain,
    w_gate,
    w_up,
    w_down,
    cotangent,
):
    factor = DH ** (-0.5)
    gathered = (
        lax.all_gather(norm1_gain, "dp", axis=0, tiled=True),
        lax.all_gather(norm2_gain, "dp", axis=0, tiled=True),
        lax.all_gather(w_query, "dp", axis=0, tiled=True),
        lax.all_gather(w_key, "dp", axis=0, tiled=True),
        lax.all_gather(w_value, "dp", axis=0, tiled=True),
        lax.all_gather(w_out, "dp", axis=1, tiled=True),
        lax.all_gather(w_gate, "dp", axis=0, tiled=True),
        lax.all_gather(w_up, "dp", axis=0, tiled=True),
        lax.all_gather(w_down, "dp", axis=1, tiled=True),
    )
    (
        gain_first,
        gain_second,
        query_full,
        key_full,
        value_full,
        out_full,
        gate_full,
        up_full,
        down_full,
    ) = gathered
    resid = tokens.astype(jnp.float32)
    first_gain = gain_first.astype(jnp.float32)
    first_scale = row_scale(resid)
    normed_first = (resid * first_scale * first_gain).astype(jnp.bfloat16)
    group_first = lax.all_gather(normed_first, "tensor", axis=0, tiled=True)
    rows = group_first.shape[0]
    heads = query_full.shape[1] // DH
    queries = (
        jnp.dot(group_first, query_full, preferred_element_type=jnp.float32)
        .astype(jnp.bfloat16)
        .reshape(rows, heads, DH)
    )
    keys = (
        jnp.dot(group_first, key_full, preferred_element_type=jnp.float32)
        .astype(jnp.bfloat16)
        .reshape(rows, heads, DH)
    )
    values = (
        jnp.dot(group_first, value_full, preferred_element_type=jnp.float32)
        .astype(jnp.bfloat16)
        .reshape(rows, heads, DH)
    )
    attended, logsum = attention_forward(queries, keys, values, seq_ids, blk_ids, factor)
    piece = attended
    attn_total = lax.psum_scatter(
        jnp.dot(piece, out_full, preferred_element_type=jnp.float32),
        "tensor",
        scatter_dimension=0,
        tiled=True,
    )
    mixed = resid + attn_total
    second_gain = gain_second.astype(jnp.float32)
    second_scale = row_scale(mixed)
    normed_second = (mixed * second_scale * second_gain).astype(jnp.bfloat16)
    group_second = lax.all_gather(normed_second, "tensor", axis=0, tiled=True)
    gate = jnp.dot(group_second, gate_full, preferred_element_type=jnp.float32)
    upward = jnp.dot(group_second, up_full, preferred_element_type=jnp.float32)
    sigmoid_gate = jax.nn.sigmoid(gate)
    silu_gate = gate * sigmoid_gate
    hidden = (silu_gate * upward).astype(jnp.bfloat16)
    piece = hidden
    ffn_total = lax.psum_scatter(
        jnp.dot(piece, down_full, preferred_element_type=jnp.float32).astype(jnp.bfloat16),
        "tensor",
        scatter_dimension=0,
        tiled=True,
    ).astype(jnp.float32)
    output = (mixed + ffn_total).astype(jnp.bfloat16)
    back_params = (
        lax.all_gather(norm1_gain, "dp", axis=0, tiled=True),
        lax.all_gather(norm2_gain, "dp", axis=0, tiled=True),
        lax.all_gather(w_query, "dp", axis=0, tiled=True),
        lax.all_gather(w_key, "dp", axis=0, tiled=True),
        lax.all_gather(w_value, "dp", axis=0, tiled=True),
        lax.all_gather(w_out, "dp", axis=1, tiled=True),
        lax.all_gather(w_gate, "dp", axis=0, tiled=True),
        lax.all_gather(w_up, "dp", axis=0, tiled=True),
        lax.all_gather(w_down, "dp", axis=1, tiled=True),
    )
    (
        back_gain_first,
        back_gain_second,
        back_query,
        back_key,
        back_value,
        back_out,
        back_gate,
        back_up,
        back_down,
    ) = back_params
    first_gain_back = back_gain_first.astype(jnp.float32)
    second_gain_back = back_gain_second.astype(jnp.float32)
    grad_rows = lax.all_gather(cotangent, "tensor", axis=0, tiled=True)
    grad_hidden = jnp.einsum("tm,fm->tf", grad_rows, back_down, preferred_element_type=jnp.float32)
    grad_down_w = jnp.einsum("tf,tm->fm", hidden, grad_rows, preferred_element_type=jnp.float32)
    slope = sigmoid_gate * (1.0 + gate * (1.0 - sigmoid_gate))
    grad_gate = (grad_hidden * upward * slope).astype(jnp.bfloat16)
    grad_upward = (grad_hidden * silu_gate).astype(jnp.bfloat16)
    grad_gate_w = jnp.einsum(
        "tm,tf->mf", group_second, grad_gate, preferred_element_type=jnp.float32
    )
    grad_up_w = jnp.einsum(
        "tm,tf->mf", group_second, grad_upward, preferred_element_type=jnp.float32
    )
    first_part = jnp.einsum("tf,mf->tm", grad_gate, back_gate, preferred_element_type=jnp.float32)
    grad_normed_second = lax.psum_scatter(
        (
            first_part
            + jnp.einsum("tf,mf->tm", grad_upward, back_up, preferred_element_type=jnp.float32)
        ).astype(jnp.bfloat16),
        "tensor",
        scatter_dimension=0,
        tiled=True,
    ).astype(jnp.float32)
    grad_mixed_norm, grad_gain_second = norm_back(
        grad_normed_second, mixed, second_scale, second_gain_back
    )
    grad_mixed = cotangent.astype(jnp.float32) + grad_mixed_norm
    attn_grad_group = lax.all_gather(grad_mixed.astype(jnp.bfloat16), "tensor", axis=0, tiled=True)
    grad_attended = jnp.einsum(
        "tm,hm->th", attn_grad_group, back_out, preferred_element_type=jnp.float32
    ).astype(jnp.bfloat16)
    grad_out_w = jnp.einsum(
        "th,tm->hm", attended, attn_grad_group, preferred_element_type=jnp.float32
    )
    grad_queries, grad_keys, grad_values = attention_backward(
        queries, keys, values, grad_attended, logsum, seq_ids, blk_ids, factor
    )
    grad_query_w = jnp.einsum(
        "tm,th->mh", group_first, grad_queries, preferred_element_type=jnp.float32
    )
    grad_key_w = jnp.einsum("tm,th->mh", group_first, grad_keys, preferred_element_type=jnp.float32)
    grad_value_w = jnp.einsum(
        "tm,th->mh", group_first, grad_values, preferred_element_type=jnp.float32
    )
    summed = (
        lax.psum_scatter(
            grad_query_w.astype(jnp.bfloat16), "dp", scatter_dimension=0, tiled=True
        ).astype(jnp.float32),
        lax.psum_scatter(
            grad_key_w.astype(jnp.bfloat16), "dp", scatter_dimension=0, tiled=True
        ).astype(jnp.float32),
        lax.psum_scatter(
            grad_value_w.astype(jnp.bfloat16), "dp", scatter_dimension=0, tiled=True
        ).astype(jnp.float32),
        lax.psum_scatter(
            grad_out_w.astype(jnp.bfloat16), "dp", scatter_dimension=1, tiled=True
        ).astype(jnp.float32),
        lax.psum_scatter(
            grad_gate_w.astype(jnp.bfloat16), "dp", scatter_dimension=0, tiled=True
        ).astype(jnp.float32),
        lax.psum_scatter(
            grad_up_w.astype(jnp.bfloat16), "dp", scatter_dimension=0, tiled=True
        ).astype(jnp.float32),
        lax.psum_scatter(
            grad_down_w.astype(jnp.bfloat16), "dp", scatter_dimension=1, tiled=True
        ).astype(jnp.float32),
    )
    grad_query_w, grad_key_w, grad_value_w, grad_out_w, grad_gate_w, grad_up_w, grad_down_w = summed
    total = jnp.einsum("th,mh->tm", grad_queries, back_query, preferred_element_type=jnp.float32)
    total = total + jnp.einsum("th,mh->tm", grad_keys, back_key, preferred_element_type=jnp.float32)
    grad_normed_first = lax.psum_scatter(
        (
            total
            + jnp.einsum("th,mh->tm", grad_values, back_value, preferred_element_type=jnp.float32)
        ).astype(jnp.bfloat16),
        "tensor",
        scatter_dimension=0,
        tiled=True,
    ).astype(jnp.float32)
    grad_tokens_norm, grad_gain_first = norm_back(
        grad_normed_first, resid, first_scale, first_gain_back
    )
    input_grad = (grad_mixed + grad_tokens_norm).astype(jnp.bfloat16)
    grad_norm_first, grad_norm_second = (
        lax.psum_scatter(grad_gain_first, ("dp", "tensor"), scatter_dimension=0, tiled=True),
        lax.psum_scatter(grad_gain_second, ("dp", "tensor"), scatter_dimension=0, tiled=True),
    )
    return (
        output,
        input_grad,
        grad_query_w,
        grad_key_w,
        grad_value_w,
        grad_out_w,
        grad_gate_w,
        grad_up_w,
        grad_down_w,
        grad_norm_first,
        grad_norm_second,
    )


def solution(mesh):
    return jax.shard_map(
        on_device,
        mesh=mesh,
        in_specs=(
            P(("dp", "tensor"), None),
            P("dp"),
            P("dp"),
            P("dp"),
            P("dp", "tensor"),
            P("dp", "tensor"),
            P("dp", "tensor"),
            P("tensor", "dp"),
            P("dp"),
            P("dp", "tensor"),
            P("dp", "tensor"),
            P("tensor", "dp"),
            P(("dp", "tensor"), None),
        ),
        out_specs=(
            P(("dp", "tensor"), None),
            P(("dp", "tensor"), None),
            P("dp", "tensor"),
            P("dp", "tensor"),
            P("dp", "tensor"),
            P("tensor", "dp"),
            P("dp", "tensor"),
            P("dp", "tensor"),
            P("tensor", "dp"),
            P(("dp", "tensor")),
            P(("dp", "tensor")),
        ),
        check_vma=False,
    )
```

profile of v0, /device:TPU:0, one launch (start us, length us, event | category | flops | bytes accessed | tf_op | source)
XLA Modules:
  0.0 1455.7 jit_solution(128816638901233754)
XLA Ops:
  10.7 6.0 all-gather
  19.0 6.5 all_gather.50
  25.5 6.1 all_gather.51
  31.6 6.1 all_gather.52
  37.7 6.1 all_gather.53
  43.7 76.2 %all-gather.10.cloned.1.call-done = bf16[3072,1024]{1,0:T(8,128)(2,1)} async-done(((bf16[384,1024]{1,0:T(8,128)(2,1)}), bf16[3072,1024]{1,0:T(8,128)(2,1)}) %all-gather.10.cloned.1.call-update) | async-done | bytes 6291472 | tf_op jit(solution)/shard_map/all_gather | solution.py:146
  119.9 5.1 convolution_convert_fusion.2
  129.7 88.6 %while.27 = (s32[]{:T(128)}, bf16[6,512,2,64]{1,3,2,0:T(8,128)(2,1)S(1)}, f32[6,2,512]{2,1,0:T(2,128)S(1)}, s32[6]{0:T(128)S(1)}, s32[3072]{0:T(1024)S(1)}, /*in...) while((s32[]{:T(128)}, ...), condition=%wide.region_4.5_spmd, body=%wide.region_1.4_spmd.sunk | while | flops 847838208 | bytes 45945020 | solution.py:49
  137.1 3.6 fusion.134
  140.7 3.8 fusion.135
  155.5 3.8 fusion.135
  166.6 3.6 fusion.134
  170.2 3.8 fusion.135
  185.0 3.8 fusion.135
  199.7 3.8 fusion.135
  214.4 3.8 fusion.135
  219.1 6.4 fusion.58
  226.1 5.1 all-gather.1
  231.2 200.0 %reduce-scatter.12.cloned.1.call-done = f32[384,1024]{1,0:T(8,128)} async-done(((f32[3072,1024]{1,0:T(8,128)}), f32[384,1024]{1,0:T(8,128)}) %reduce-scatter.12.cloned.1.call-update) | async-done | bytes 1572880 | tf_op jit(solution)/shard_map/reduce_scatter | solution.py:166
  436.8 95.5 %all-gather.12.cloned.1.call-done = bf16[3072,1024]{1,0:T(8,128)(2,1)} async-done(((bf16[384,1024]{1,0:T(8,128)(2,1)}), bf16[3072,1024]{1,0:T(8,128)(2,1)}) %all-gather.12.cloned.1.call-update) | async-done | bytes 6291472 | tf_op jit(solution)/shard_map/all_gather | solution.py:176
  532.3 9.1 fusion.60
  541.5 7.1 all-gather.14.cloned.1.call-done
  548.5 9.1 fusion.59
  557.6 9.2 all-gather.18.cloned.1.call-done
  566.8 101.0 %all-gather.20.cloned.1.call-done = bf16[3072,1024]{1,0:T(8,128)(2,1)} async-done(((bf16[384,1024]{1,0:T(8,128)(2,1)}), bf16[3072,1024]{1,0:T(8,128)(2,1)}) %all-gather.20.cloned.1.call-update) | async-done | bytes 6291472 | tf_op jit(solution)/shard_map/all_gather | solution.py:214
  667.8 14.8 %multiply_convert_fusion.1 = (bf16[3072,512]{1,0:T(8,128)(2,1)}, bf16[3072,512]{1,0:T(8,128)(2,1)}, bf16[3072,512]{1,0:T(8,128)(2,1)}) fusion(f32[3072,512]{1,0:T(8,128)} %fusion.59, f32[3072,512]{1,0:T(8,128)} %fusion.60, bf16[3072,1024]{1,0:T(8,128)(2,1)} %all-gather.20.cloned.1.call-done, bf16[512,1024]{1,0:T(8,128)(2,1)} %all-gather.18.cloned.1.call-done), kind=kOutput, calls=%fused_computation.47 | convolution fusion | flops 3244818432 | bytes 29360128 | tf_op jit(solution)/shard_map/tm,fm->tf/dot_general | solution.py:215
  682.7 5.7 fusion.61
  688.4 7.7 add_convert_fusion.1
  696.1 115.9 %reduce-scatter.16.cloned.1.call-done = bf16[384,1024]{1,0:T(8,128)(2,1)} async-done(((bf16[3072,1024]{1,0:T(8,128)(2,1)}), bf16[384,1024]{1,0:T(8,128)(2,1)}) %reduce-scatter.16.cloned.1.call-update) | async-done | bytes 786448 | tf_op jit(solution)/shard_map/reduce_scatter | solution.py:227
  817.6 8.1 convolution_convert_fusion.5
  826.0 8.2 convolution_convert_fusion.6
  834.3 8.2 convolution_convert_fusion.7
  842.6 73.4 %all-gather.22.cloned.1.call-done = bf16[3072,1024]{1,0:T(8,128)(2,1)} async-done(((bf16[384,1024]{1,0:T(8,128)(2,1)}), bf16[3072,1024]{1,0:T(8,128)(2,1)}) %all-gather.22.cloned.1.call-update) | async-done | bytes 6291472 | tf_op jit(solution)/shard_map/all_gather | solution.py:240
  916.0 4.7 convolution_convert_fusion.8
  920.8 5.9 convolution_convert_fusion.1
  927.7 201.2 %while.28 = (s32[]{:T(128)}, f32[3072,2,64]{0,2,1:T(8,128)S(1)}, f32[3072,2,64]{0,2,1:T(8,128)}, bf16[6,512,2,64]{1,3,2,0:T(8,128)(2,1)}, s32[6]{0:T(128)S(1)}, ...) while((s32[]{:T(128)}, f32[3072,2,64]{0,2,1:T(8,128)S(1)}, ...), condition=%wide.region_12.13_spmd.clone, body=%wide.region_10.12_spmd.clone.sunk | while | flops 2067266560 | bytes 122618160 | solution.py:96
  935.1 4.8 fusion.147
  939.9 8.9 multiply_reduce_fusion.3
  948.8 7.5 multiply_convert_fusion.6
  968.5 4.8 fusion.147
  973.3 8.9 multiply_reduce_fusion.3
  982.3 7.5 multiply_convert_fusion.6
  1002.0 4.8 fusion.147
  1006.8 8.9 multiply_reduce_fusion.3
  1015.7 7.5 multiply_convert_fusion.6
  1035.5 4.8 fusion.147
  1040.3 8.9 multiply_reduce_fusion.3
  1049.2 7.5 multiply_convert_fusion.6
  1069.0 4.8 fusion.147
  1073.8 8.9 multiply_reduce_fusion.3
  1082.7 7.5 multiply_convert_fusion.6
  1102.5 4.7 fusion.147
  1107.2 8.9 multiply_reduce_fusion.3
  1116.1 7.5 multiply_convert_fusion.6
  1131.8 5.5 convolution_convert_fusion.11
  1137.3 7.6 fusion.63
  1147.7 6.4 fusion.62
  1154.2 5.3 convolution_convert_fusion.9
  1159.6 12.2 add_convert_fusion
  1173.0 7.6 convolution_convert_fusion
  1190.8 10.3 reduce-scatter.24.cloned.1.call-done
  1202.6 120.1 %reduce-scatter.18.cloned.1.call-done = bf16[384,1024]{1,0:T(8,128)(2,1)} async-done(((bf16[3072,1024]{1,0:T(8,128)(2,1)}), bf16[384,1024]{1,0:T(8,128)(2,1)}) %reduce-scatter.18.cloned.1.call-update) | async-done | bytes 786448 | tf_op jit(solution)/shard_map/reduce_scatter | solution.py:283
  1324.4 42.2 %all-reduce.2 = (f32[1024]{0:T(1024)S(1)}, f32[1024]{0:T(1024)S(1)}) all-reduce(f32[1024]{0:T(1024)S(1)} %get-tuple-element.169, f32[1024]{0:T(1024)S(1)} %copy-done.31), channel_id=13, replica_groups=mesh['dp'=4,'tensor'=8] {'dp','tensor'}, use_global_device_ids=true, to_apply=%region_23.24.clone | all-reduce | flops 2048 | bytes 16384
  1367.8 76.8 %reduce-scatter.14.cloned.1.call-done = bf16[384,1024]{1,0:T(8,128)(2,1)} async-done(((bf16[3072,1024]{1,0:T(8,128)(2,1)}), bf16[384,1024]{1,0:T(8,128)(2,1)}) %reduce-scatter.14.cloned.1.call-update) | async-done | bytes 786448 | tf_op jit(solution)/shard_map/reduce_scatter | solution.py:183
  (270 shorter events, 156.1 us)
Async XLA Ops:
  8.0 111.9 %all-gather.10.cloned.1.call-start = ((), (), s32[]{:S(2)}) async-start(), calls=%async_computation.11 | async-start | bytes 7077888 | tf_op jit(solution)/shard_map/all_gather | solution.py:146
  10.7 14.8 %copy-start.25 = (f32[384]{0:T(512)}, f32[384]{0:T(512)S(1)}, u32[]{:S(2)}) copy-start(f32[384]{0:T(512)S(1)} %get-tuple-element.227) | copy-start | bytes 4612
  16.7 8.8 copy-start.21
  19.0 412.2 %reduce-scatter.12.cloned.1.call-start = ((), (), s32[]{:S(2)}) async-start(), calls=%async_computation.12 | async-start | bytes 14155776 | tf_op jit(solution)/shard_map/reduce_scatter | solution.py:166
  25.5 101.8 %copy-start.10 = (bf16[1024,128]{1,0:T(8,128)(2,1)}, bf16[1024,128]{1,0:T(8,128)(2,1)S(1)}, u32[]{:S(2)}) copy-start(bf16[1024,128]{1,0:T(8,128)(2,1)S(1)} %all_gather.50) | copy-start | bytes 786436
  31.6 93.5 %copy-start.12 = (bf16[1024,128]{1,0:T(8,128)(2,1)}, bf16[1024,128]{1,0:T(8,128)(2,1)S(1)}, u32[]{:S(2)}) copy-start(bf16[1024,128]{1,0:T(8,128)(2,1)S(1)} %all_gather.51) | copy-start | bytes 786436
  37.7 82.3 %copy-start.8 = (bf16[1024,128]{1,0:T(8,128)(2,1)}, bf16[1024,128]{1,0:T(8,128)(2,1)S(1)}, u32[]{:S(2)}) copy-start(bf16[1024,128]{1,0:T(8,128)(2,1)S(1)} %all_gather.52) | copy-start | bytes 786436
  119.9 5.2 copy-start
  127.3 2.3 copy-start.14
  127.3 2.3 copy-start.15
  218.3 7.1 copy-start.4
  219.1 6.4 copy-start.5
  225.4 211.4 %all-gather.16.cloned.1.call-start = ((), (), s32[]{:S(2)}) async-start(), calls=%async_computation.15 | async-start | bytes 1310720 | tf_op jit(solution)/shard_map/all_gather | solution.py:128
  226.0 306.3 %all-gather.12.cloned.1.call-start = ((), (), s32[]{:S(2)}) async-start(), calls=%async_computation.13 | async-start | bytes 7077888 | tf_op jit(solution)/shard_map/all_gather | solution.py:176
  231.2 583.1 %copy-start.19 = (f32[4,1,256]{2,1,0:T(1,128)}, f32[4,1,256]{2,1,0:T(1,128)S(1)}, u32[]{:S(2)}) copy-start(f32[4,1,256]{2,1,0:T(1,128)S(1)} %convert_element_type.176) | copy-start | bytes 12292
  433.1 381.2 %copy-start.1 = (f32[384,1024]{1,0:T(8,128)}, f32[384,1024]{1,0:T(8,128)S(1)}, u32[]{:S(2)}) copy-start(f32[384,1024]{1,0:T(8,128)S(1)} %get-tuple-element.216) | copy-start | bytes 4718596
  433.1 381.2 %copy-start.23 = (f32[384]{0:T(512)}, f32[384]{0:T(512)S(1)}, u32[]{:S(2)}) copy-start(f32[384]{0:T(512)S(1)} %get-tuple-element.229) | copy-start | bytes 4612
  433.1 381.2 %copy-start.27 = (f32[384]{0:T(512)}, f32[384]{0:T(512)S(1)}, u32[]{:S(2)}) copy-start(f32[384]{0:T(512)S(1)} %get-tuple-element.228) | copy-start | bytes 4612
  434.4 114.1 %all-gather.14.cloned.1.call-start = ((), (), s32[]{:S(2)}) async-start(), calls=%async_computation.14 | async-start | bytes 1310720 | tf_op jit(solution)/shard_map/all_gather | solution.py:127
  435.0 131.9 %all-gather.18.cloned.1.call-start = ((), (), s32[]{:S(2)}) async-start(), calls=%async_computation.16 | async-start | bytes 1310720 | tf_op jit(solution)/shard_map/all_gather | solution.py:129
  435.7 232.1 %all-gather.20.cloned.1.call-start = ((), (), s32[]{:S(2)}) async-start(), calls=%async_computation.18 | async-start | bytes 7077888 | tf_op jit(solution)/shard_map/all_gather | solution.py:214
  436.5 375.5 %reduce-scatter.16.cloned.1.call-start = ((), (), s32[]{:S(2)}) async-start(), calls=%async_computation.19 | async-start | bytes 7077888 | tf_op jit(solution)/shard_map/reduce_scatter | solution.py:227
  667.8 14.8 %copy-start.35 = (bf16[1024,512]{1,0:T(8,128)(2,1)S(1)}, bf16[1024,512]{1,0:T(8,128)(2,1)}, u32[]{:S(2)}) copy-start(bf16[1024,512]{1,0:T(8,128)(2,1)} %all-gather.14.cloned.1.call-done) | copy-start | bytes 3145732
  682.6 5.7 copy-start.34
  696.1 219.9 %all-gather.22.cloned.1.call-start = ((), (), s32[]{:S(2)}) async-start(), calls=%async_computation.20 | async-start | bytes 7077888 | tf_op jit(solution)/shard_map/all_gather | solution.py:240
  817.6 363.2 %reduce-scatter.32.cloned.1.call-start = ((), (), s32[]{:S(2)}) async-start(), calls=%async_computation.28 | async-start | bytes 1310720 | tf_op jit(solution)/shard_map/reduce_scatter | solution.py:276
  825.8 356.9 %reduce-scatter.30.cloned.1.call-start = ((), (), s32[]{:S(2)}) async-start(), calls=%async_computation.27 | async-start | bytes 1310720 | tf_op jit(solution)/shard_map/reduce_scatter | solution.py:273
  834.3 350.2 %reduce-scatter.28.cloned.1.call-start = ((), (), s32[]{:S(2)}) async-start(), calls=%async_computation.26 | async-start | bytes 1310720 | tf_op jit(solution)/shard_map/reduce_scatter | solution.py:270
  842.5 343.8 %reduce-scatter.26.cloned.1.call-start = ((), (), s32[]{:S(2)}) async-start(), calls=%async_computation.25 | async-start | bytes 327680 | tf_op jit(solution)/shard_map/reduce_scatter | solution.py:267
  920.8 267.1 %reduce-scatter.20.cloned.1.call-start = ((), (), s32[]{:S(2)}) async-start(), calls=%async_computation.22 | async-start | bytes 327680 | tf_op jit(solution)/shard_map/reduce_scatter | solution.py:258
  932.1 3.0 copy-start.16
  939.8 8.9 copy-start.17
  965.5 3.0 copy-start.16
  973.3 8.9 copy-start.17
  999.0 3.0 copy-start.16
  1006.8 8.9 copy-start.17
  1032.5 3.0 copy-start.16
  1040.3 8.9 copy-start.17
  1066.0 3.0 copy-start.16
  1073.8 8.9 copy-start.17
  1099.5 3.0 copy-start.16
  1107.2 8.9 copy-start.17
  1130.5 6.8 copy-start.13
  1131.8 13.2 slice-start
  1137.3 52.0 %reduce-scatter.22.cloned.1.call-start = ((), (), s32[]{:S(2)}) async-start(), calls=%async_computation.23 | async-start | bytes 327680 | tf_op jit(solution)/shard_map/reduce_scatter | solution.py:261
  1137.3 7.7 slice-start.1
  1137.3 7.7 copy-start.7
  1145.0 2.7 copy-start.11
  1147.6 6.4 copy-start.18
  1147.6 53.5 %reduce-scatter.24.cloned.1.call-start = ((), (), s32[]{:S(2)}) async-start(), calls=%async_computation.24 | async-start | bytes 327680 | tf_op jit(solution)/shard_map/reduce_scatter | solution.py:264
  1154.1 5.5 copy-start.9
  1159.5 163.2 %reduce-scatter.18.cloned.1.call-start = ((), (), s32[]{:S(2)}) async-start(), calls=%async_computation.21 | async-start | bytes 7077888 | tf_op jit(solution)/shard_map/reduce_scatter | solution.py:283
  1171.8 272.8 %reduce-scatter.14.cloned.1.call-start = ((), (), s32[]{:S(2)}) async-start(), calls=%async_computation.17 | async-start | bytes 7077888 | tf_op jit(solution)/shard_map/reduce_scatter | solution.py:183
  1180.6 142.1 %copy-start.3 = (bf16[384,1024]{1,0:T(8,128)(2,1)S(1)}, bf16[384,1024]{1,0:T(8,128)(2,1)}, u32[]{:S(2)}) copy-start(bf16[384,1024]{1,0:T(8,128)(2,1)} %param.17) | copy-start | bytes 2359300
  1180.6 142.1 %copy-start.22 = (f32[4,1,256]{2,1,0:T(1,128)S(1)}, f32[4,1,256]{2,1,0:T(1,128)}, u32[]{:S(2)}) copy-start(f32[4,1,256]{2,1,0:T(1,128)} %copy-done.21) | copy-start | bytes 12292
  1180.6 142.1 %copy-start.26 = (f32[384]{0:T(512)S(1)}, f32[384]{0:T(512)}, u32[]{:S(2)}) copy-start(f32[384]{0:T(512)} %copy-done.25) | copy-start | bytes 4612
  1180.6 143.8 %copy-start.31 = (f32[1024]{0:T(1024)S(1)}, f32[1024]{0:T(1024)}, u32[]{:S(2)}) copy-start(f32[1024]{0:T(1024)} %get-tuple-element.167) | copy-start | bytes 12292
  1180.6 264.0 %copy-start.2 = (f32[384,1024]{1,0:T(8,128)S(1)}, f32[384,1024]{1,0:T(8,128)}, u32[]{:S(2)}) copy-start(f32[384,1024]{1,0:T(8,128)} %copy-done.1) | copy-start | bytes 4718596
  1180.6 264.0 %copy-start.6 = (bf16[384,1024]{1,0:T(8,128)(2,1)S(1)}, bf16[384,1024]{1,0:T(8,128)(2,1)}, u32[]{:S(2)}) copy-start(bf16[384,1024]{1,0:T(8,128)(2,1)} %param.29) | copy-start | bytes 2359300
  1180.6 264.0 %copy-start.20 = (f32[4,1,256]{2,1,0:T(1,128)S(1)}, f32[4,1,256]{2,1,0:T(1,128)}, u32[]{:S(2)}) copy-start(f32[4,1,256]{2,1,0:T(1,128)} %copy-done.19) | copy-start | bytes 12292
  1180.7 264.0 %copy-start.24 = (f32[384]{0:T(512)S(1)}, f32[384]{0:T(512)}, u32[]{:S(2)}) copy-start(f32[384]{0:T(512)} %copy-done.23) | copy-start | bytes 4612
  1180.7 264.0 %copy-start.28 = (f32[384]{0:T(512)S(1)}, f32[384]{0:T(512)}, u32[]{:S(2)}) copy-start(f32[384]{0:T(512)} %copy-done.27) | copy-start | bytes 4612
  1180.7 264.0 %copy-start.30 = (f32[384]{0:T(512)S(1)}, f32[384]{0:T(512)}, u32[]{:S(2)}) copy-start(f32[384]{0:T(512)} %copy-done.29) | copy-start | bytes 4612
  1180.7 264.0 %copy-start.32 = (f32[384]{0:T(512)S(1)}, f32[384]{0:T(512)}, u32[]{:S(2)}) copy-start(f32[384]{0:T(512)} %get-tuple-element.226) | copy-start | bytes 4612
  (3 other events, 2.5 us)
Sparse Core Ops, SparseCore 0:
  19.1 100.8 all-gather.9
  225.6 205.5 reduce-scatter.11
  817.7 98.2 all-gather.21
Sparse Core Ops, SparseCore 1:
  227.5 14.8 all-gather.15
  434.5 97.8 all-gather.11
  533.8 14.7 all-gather.13
  550.1 16.7 all-gather.17
  569.1 98.7 all-gather.19
  696.2 115.8 reduce-scatter.15
  825.9 24.1 reduce-scatter.31
  852.5 24.8 reduce-scatter.29
  879.8 24.9 reduce-scatter.27
  920.8 18.2 reduce-scatter.25
  1137.3 18.1 reduce-scatter.19
  1158.7 20.0 reduce-scatter.21
  1181.1 20.0 reduce-scatter.23
  1205.1 117.5 reduce-scatter.17
  1326.7 117.8 reduce-scatter.13
where the time goes:
time: 1460 us
  waiting for transfers between devices  888 us (61%)
  matrix products  316 us (22%)
  other arithmetic  115 us (8%)
  blocking collectives  77.9 us (5%)
  loops' own time  24.7 us (2%)
  between operations  16.6 us (1%)
  local copies, waits for them, and re-layouts  16.3 us (1%)
    reduce_scatter x1, waiting for transfers between devices, on_device(): lax.psum_scatter(jnp.dot(piece, out_full, preferred_element_type=jnp.floa...  200 us
    reduce_scatter x1, waiting for transfers between devices, on_device(): lax.psum_scatter((total + jnp.einsum('th,mh->tm', grad_values, back_value...  120 us
    reduce_scatter x1, waiting for transfers between devices, on_device(): lax.psum_scatter((first_part + jnp.einsum('tf,mf->tm', grad_upward, back_...  116 us
    all_gather x1, waiting for transfers between devices, on_device(): grad_rows = lax.all_gather(cotangent, 'tensor', axis=0, tiled=True)  101 us
    all_gather x1, waiting for transfers between devices, on_device(): group_second = lax.all_gather(normed_second, 'tensor', axis=0, tiled=True)  95.5 us
    reduce_scatter x1, waiting for transfers between devices, on_device(): lax.psum_scatter(jnp.dot(piece, down_full, preferred_element_type=jnp.flo...  76.8 us
    all_gather x1, waiting for transfers between devices, on_device(): group_first = lax.all_gather(normed_first, 'tensor', axis=0, tiled=True)  76.2 us
    all_gather x1, waiting for transfers between devices, on_device(): lax.all_gather(grad_mixed.astype(jnp.bfloat16), 'tensor', axis=0, tiled=T...  73.4 us
  transfers between devices with their start and end apart: 18, of which 11 were waited for; matrix products, arithmetic and copies ran while one was open for 21% of the time, Pallas kernels for 0%

commit v1 on v0

--- a/solution.py
+++ b/solution.py
@@ -173,7 +173,35 @@
     second_gain = gain_second.astype(jnp.float32)
     second_scale = row_scale(mixed)
     normed_second = (mixed * second_scale * second_gain).astype(jnp.bfloat16)
-    group_second = lax.all_gather(normed_second, "tensor", axis=0, tiled=True)
+    n_now, met_up, v_now = (
+        jax.lax.axis_size("tensor"),
+        jax.lax.axis_index("tensor"),
+        normed_second.shape[0],
+    )
+    seen = []
+    for i in tuple(range(n_now)):
+        seen.append((i, (i + 1) % n_now))
+    column = []
+    for i in [*range(n_now)]:
+        column.append((i, (i - 1) % n_now))
+    group_second = jnp.zeros(
+        (*normed_second.shape[:0], n_now * v_now, *normed_second.shape[1:]), normed_second.dtype
+    )
+    group_second = lax.dynamic_update_slice_in_dim(
+        group_second, normed_second, met_up * v_now, axis=0
+    )
+    y1 = u_next = normed_second
+    outer = n_now // 2
+    for p in [*range(1, outer + 1)]:
+        y1 = jax.lax.ppermute(y1, axis_name="tensor", perm=seen)
+        group_second = lax.dynamic_update_slice_in_dim(
+            group_second, y1, (met_up - p) % n_now * v_now, axis=0
+        )
+        if p < n_now - outer:
+            u_next = jax.lax.ppermute(u_next, axis_name="tensor", perm=column)
+            group_second = lax.dynamic_update_slice_in_dim(
+                group_second, u_next, (met_up + p) % n_now * v_now, axis=0
+            )
     gate = jnp.dot(group_second, gate_full, preferred_element_type=jnp.float32)
     upward = jnp.dot(group_second, up_full, preferred_element_type=jnp.float32)
     sigmoid_gate = jax.nn.sigmoid(gate)

time: 1460 us -> 1410 us (0.966)
  waiting for transfers between devices: 888 us -> 807 us
  local copies, waits for them, and re-layouts: 16.3 us -> 33.3 us
  starting transfers between devices: 1.19 us -> 17.7 us
    all_gather x1, waiting for transfers between devices: 101 us -> 0.01 us  [on_device(): grad_rows = lax.all_gather(cotangent, 'tensor', axis=0, tiled=True)]
    all_gather x1 -> x0, waiting for transfers between devices: 95.5 us -> none  [on_device(): group_second = lax.all_gather(normed_second, 'tensor', axis=0, tiled=True)]
    ppermute x0 -> x7, waiting for transfers between devices: none -> 89.5 us  [the longest x4 89.5 us: on_device(): y1 = jax.lax.ppermute(y1, axis_name='tensor', perm=seen)]
    reduce_scatter x1, waiting for transfers between devices: 200 us -> 244 us  [on_device(): lax.psum_scatter(jnp.dot(piece, out_full, preferred_element_type=jnp.floa...]
    ppermute x0 -> x7, starting transfers between devices: none -> 16.8 us  [the longest x4 9.24 us: on_device(): y1 = jax.lax.ppermute(y1, axis_name='tensor', perm=seen)]
  transfers between devices with their start and end apart: 18 -> 24, of which waited for: 11 -> 11; matrix products, arithmetic and copies ran while one was open for 21% -> 23% of each run, Pallas kernels for 0% -> 0%
where the time goes in v1:
time: 1410 us; the launch traced here: 1400 us
  waiting for transfers between devices  807 us (57%)
  matrix products  313 us (22%)
  other arithmetic  115 us (8%)
  blocking collectives  77.8 us (6%)
  local copies, waits for them, and re-layouts  33.3 us (2%)
  loops' own time  25.1 us (2%)
  starting transfers between devices  17.7 us (1%)
  between operations  16.7 us (1%)
    reduce_scatter x1, waiting for transfers between devices, on_device(): lax.psum_scatter(jnp.dot(piece, out_full, preferred_element_type=jnp.floa...  244 us
    reduce_scatter x1, waiting for transfers between devices, on_device(): lax.psum_scatter((total + jnp.einsum('th,mh->tm', grad_values, back_value...  120 us
    reduce_scatter x1, waiting for transfers between devices, on_device(): lax.psum_scatter((first_part + jnp.einsum('tf,mf->tm', grad_upward, back_...  115 us
    ppermute x4, waiting for transfers between devices, on_device(): y1 = jax.lax.ppermute(y1, axis_name='tensor', perm=seen)  89.5 us
    reduce_scatter x1, waiting for transfers between devices, on_device(): lax.psum_scatter(jnp.dot(piece, down_full, preferred_element_type=jnp.flo...  77 us
    all_gather x1, waiting for transfers between devices, on_device(): group_first = lax.all_gather(normed_first, 'tensor', axis=0, tiled=True)  76.2 us
    all_gather x1, waiting for transfers between devices, on_device(): lax.all_gather(grad_mixed.astype(jnp.bfloat16), 'tensor', axis=0, tiled=T...  73.2 us
    dot_general x6, matrix products, one_block(): jnp.einsum('qhd,khd->hqk', grad_block, values, preferred_element_type=jnp...  53.4 us
  transfers between devices with their start and end apart: 24, of which 11 were waited for; matrix products, arithmetic and copies ran while one was open for 23% of the time, Pallas kernels for 0%

profile of v1, /device:TPU:0, one launch (start us, length us, event | category | flops | bytes accessed | tf_op | source)
XLA Modules:
  0.0 1405.0 jit_solution(15061850655788084513)
XLA Ops:
  10.7 6.0 all-gather
  19.0 6.5 all_gather.47
  25.5 6.1 all_gather.48
  31.6 6.1 all_gather.49
  37.7 6.1 all_gather.50
  43.7 76.2 %all-gather.9.cloned.1.call-done = bf16[3072,1024]{1,0:T(8,128)(2,1)} async-done(((bf16[384,1024]{1,0:T(8,128)(2,1)}), bf16[3072,1024]{1,0:T(8,128)(2,1)}) %all-gather.9.cloned.1.call-update) | async-done | bytes 6291472 | tf_op jit(solution)/shard_map/all_gather | solution.py:146
  119.9 5.1 convolution_convert_fusion.2
  129.7 88.9 %while.27 = (s32[]{:T(128)}, bf16[6,512,2,64]{1,3,2,0:T(8,128)(2,1)S(1)}, f32[6,2,512]{2,1,0:T(2,128)S(1)}, s32[6]{0:T(128)S(1)}, s32[3072]{0:T(1024)S(1)}, /*in...) while((s32[]{:T(128)}, ...), condition=%wide.region_4.5_spmd, body=%wide.region_1.4_spmd.sunk | while | flops 847838208 | bytes 45945020 | solution.py:49
  141.0 3.8 fusion.135
  152.1 3.6 fusion.134
  155.7 3.8 fusion.135
  166.8 3.6 fusion.134
  170.5 3.8 fusion.135
  181.6 3.6 fusion.134
  185.2 3.8 fusion.135
  199.9 3.8 fusion.135
  214.7 3.8 fusion.135
  219.3 6.4 fusion.58
  227.6 5.1 all-gather.1
  232.6 244.0 %reduce-scatter.12.cloned.1.call-done = f32[384,1024]{1,0:T(8,128)} async-done(((f32[3072,1024]{1,0:T(8,128)}), f32[384,1024]{1,0:T(8,128)}) %reduce-scatter.12.cloned.1.call-update) | async-done | bytes 1572880 | tf_op jit(solution)/shard_map/reduce_scatter | solution.py:166
  487.9 30.5 %collective-permute-done = bf16[384,1024]{1,0:T(8,128)(2,1)} collective-permute-done((bf16[384,1024]{1,0:T(8,128)(2,1)S(1)}, bf16[384,1024]{1,0:T(8,128)(2,1)}, u32[]{:S(2)}, u32[]{:S(2)}) %collective-permute-start) | collective-permute-done | bytes 786464 | tf_op jit(solution)/shard_map/ppermute | solution.py:196
  523.4 30.9 %collective-permute-done.2 = bf16[384,1024]{1,0:T(8,128)(2,1)} collective-permute-done((bf16[384,1024]{1,0:T(8,128)(2,1)}, bf16[384,1024]{1,0:T(8,128)(2,1)}, u32[]{:S(2)}, u32[]{:S(2)}) %collective-permute-start.2) | collective-permute-done | bytes 786464 | tf_op jit(solution)/shard_map/ppermute | solution.py:196
  559.0 9.2 fusion.60
  568.2 21.7 %collective-permute-done.4 = bf16[384,1024]{1,0:T(8,128)(2,1)} collective-permute-done((bf16[384,1024]{1,0:T(8,128)(2,1)}, bf16[384,1024]{1,0:T(8,128)(2,1)}, u32[]{:S(2)}, u32[]{:S(2)}) %collective-permute-start.4) | collective-permute-done | bytes 786464 | tf_op jit(solution)/shard_map/ppermute | solution.py:196
  605.2 6.3 collective-permute-done.6
  612.4 9.2 fusion.59
  621.6 13.5 multiply_convert_fusion.1
  638.5 7.7 add_convert_fusion.1
  646.5 114.7 %reduce-scatter.16.cloned.1.call-done = bf16[384,1024]{1,0:T(8,128)(2,1)} async-done(((bf16[3072,1024]{1,0:T(8,128)(2,1)}), bf16[384,1024]{1,0:T(8,128)(2,1)}) %reduce-scatter.16.cloned.1.call-update) | async-done | bytes 786448 | tf_op jit(solution)/shard_map/reduce_scatter | solution.py:255
  766.8 8.1 convolution_convert_fusion.5
  775.0 8.3 convolution_convert_fusion.6
  783.4 8.3 convolution_convert_fusion.7
  791.8 73.2 %all-gather.19.cloned.1.call-done = bf16[3072,1024]{1,0:T(8,128)(2,1)} async-done(((bf16[384,1024]{1,0:T(8,128)(2,1)}), bf16[3072,1024]{1,0:T(8,128)(2,1)}) %all-gather.19.cloned.1.call-update) | async-done | bytes 6291472 | tf_op jit(solution)/shard_map/all_gather | solution.py:268
  864.9 4.7 convolution_convert_fusion.8
  869.7 6.1 convolution_convert_fusion.1
  876.7 201.5 %while.28 = (s32[]{:T(128)}, f32[3072,2,64]{0,2,1:T(8,128)S(1)}, f32[3072,2,64]{0,2,1:T(8,128)}, bf16[6,512,2,64]{1,3,2,0:T(8,128)(2,1)}, s32[6]{0:T(128)S(1)}, ...) while((s32[]{:T(128)}, f32[3072,2,64]{0,2,1:T(8,128)S(1)}, ...), condition=%wide.region_12.13_spmd.clone, body=%wide.region_10.12_spmd.clone.sunk | while | flops 2067266560 | bytes 122618160 | solution.py:96
  884.4 4.8 fusion.147
  889.1 8.9 multiply_reduce_fusion.3
  898.1 7.6 multiply_convert_fusion.7
  917.9 4.8 fusion.147
  922.7 8.9 multiply_reduce_fusion.3
  931.6 7.6 multiply_convert_fusion.7
  951.6 4.8 fusion.147
  956.3 8.9 multiply_reduce_fusion.3
  965.3 7.5 multiply_convert_fusion.7
  985.0 4.8 fusion.147
  989.8 8.9 multiply_reduce_fusion.3
  998.7 7.5 multiply_convert_fusion.7
  1018.5 4.8 fusion.147
  1023.3 8.9 multiply_reduce_fusion.3
  1032.2 7.5 multiply_convert_fusion.7
  1052.0 4.7 fusion.147
  1056.7 8.8 multiply_reduce_fusion.3
  1065.6 7.5 multiply_convert_fusion.7
  1081.2 5.5 convolution_convert_fusion.11
  1086.8 7.7 fusion.63
  1097.1 6.4 fusion.62
  1103.6 5.3 convolution_convert_fusion.9
  1109.0 12.2 add_convert_fusion
  1122.5 7.5 convolution_convert_fusion
  1140.2 10.2 reduce-scatter.24.cloned.1.call-done
  1151.9 120.2 %reduce-scatter.18.cloned.1.call-done = bf16[384,1024]{1,0:T(8,128)(2,1)} async-done(((bf16[3072,1024]{1,0:T(8,128)(2,1)}), bf16[384,1024]{1,0:T(8,128)(2,1)}) %reduce-scatter.18.cloned.1.call-update) | async-done | bytes 786448 | tf_op jit(solution)/shard_map/reduce_scatter | solution.py:311
  1273.7 42.1 %all-reduce.2 = (f32[1024]{0:T(1024)S(1)}, f32[1024]{0:T(1024)S(1)}) all-reduce(f32[1024]{0:T(1024)S(1)} %get-tuple-element.169, f32[1024]{0:T(1024)S(1)} %copy-done.31), channel_id=13, replica_groups=mesh['dp'=4,'tensor'=8] {'dp','tensor'}, use_global_device_ids=true, to_apply=%region_23.24.clone | all-reduce | flops 2048 | bytes 16384
  1317.0 77.0 %reduce-scatter.14.cloned.1.call-done = bf16[384,1024]{1,0:T(8,128)(2,1)} async-done(((bf16[3072,1024]{1,0:T(8,128)(2,1)}), bf16[384,1024]{1,0:T(8,128)(2,1)}) %reduce-scatter.14.cloned.1.call-update) | async-done | bytes 786448 | tf_op jit(solution)/shard_map/reduce_scatter | solution.py:211
  (291 shorter events, 188.5 us)
Async XLA Ops:
  8.0 111.9 %all-gather.9.cloned.1.call-start = ((), (), s32[]{:S(2)}) async-start(), calls=%async_computation.11 | async-start | bytes 7077888 | tf_op jit(solution)/shard_map/all_gather | solution.py:146
  10.7 14.8 %copy-start.25 = (f32[384]{0:T(512)}, f32[384]{0:T(512)S(1)}, u32[]{:S(2)}) copy-start(f32[384]{0:T(512)S(1)} %get-tuple-element.229) | copy-start | bytes 4612
  16.7 8.8 copy-start.21
  18.9 457.7 %reduce-scatter.12.cloned.1.call-start = ((), (), s32[]{:S(2)}) async-start(), calls=%async_computation.12 | async-start | bytes 14155776 | tf_op jit(solution)/shard_map/reduce_scatter | solution.py:166
  25.5 101.8 %copy-start.10 = (bf16[1024,128]{1,0:T(8,128)(2,1)}, bf16[1024,128]{1,0:T(8,128)(2,1)S(1)}, u32[]{:S(2)}) copy-start(bf16[1024,128]{1,0:T(8,128)(2,1)S(1)} %all_gather.47) | copy-start | bytes 786436
  31.6 93.5 %copy-start.12 = (bf16[1024,128]{1,0:T(8,128)(2,1)}, bf16[1024,128]{1,0:T(8,128)(2,1)S(1)}, u32[]{:S(2)}) copy-start(bf16[1024,128]{1,0:T(8,128)(2,1)S(1)} %all_gather.48) | copy-start | bytes 786436
  37.7 82.3 %copy-start.8 = (bf16[1024,128]{1,0:T(8,128)(2,1)}, bf16[1024,128]{1,0:T(8,128)(2,1)S(1)}, u32[]{:S(2)}) copy-start(bf16[1024,128]{1,0:T(8,128)(2,1)S(1)} %all_gather.49) | copy-start | bytes 786436
  119.9 5.2 copy-start
  218.5 7.2 copy-start.4
  219.3 6.4 copy-start.5
  225.7 333.2 %all-gather.15.cloned.1.call-start = ((), (), s32[]{:S(2)}) async-start(), calls=%async_computation.15 | async-start | bytes 1310720 | tf_op jit(solution)/shard_map/all_gather | solution.py:129
  226.3 332.7 %all-gather.17.cloned.1.call-start = ((), (), s32[]{:S(2)}) async-start(), calls=%async_computation.17 | async-start | bytes 7077888 | tf_op jit(solution)/shard_map/all_gather | solution.py:242
  226.9 385.5 %all-gather.13.cloned.1.call-start = ((), (), s32[]{:S(2)}) async-start(), calls=%async_computation.14 | async-start | bytes 1310720 | tf_op jit(solution)/shard_map/all_gather | solution.py:128
  227.5 394.1 %all-gather.11.cloned.1.call-start = ((), (), s32[]{:S(2)}) async-start(), calls=%async_computation.13 | async-start | bytes 1310720 | tf_op jit(solution)/shard_map/all_gather | solution.py:127
  232.6 530.8 %copy-start.19 = (f32[4,1,256]{2,1,0:T(1,128)}, f32[4,1,256]{2,1,0:T(1,128)S(1)}, u32[]{:S(2)}) copy-start(f32[4,1,256]{2,1,0:T(1,128)S(1)} %convert_element_type.176) | copy-start | bytes 12292
  478.5 284.9 %copy-start.1 = (f32[384,1024]{1,0:T(8,128)}, f32[384,1024]{1,0:T(8,128)S(1)}, u32[]{:S(2)}) copy-start(f32[384,1024]{1,0:T(8,128)S(1)} %get-tuple-element.218) | copy-start | bytes 4718596
  478.5 284.9 %copy-start.23 = (f32[384]{0:T(512)}, f32[384]{0:T(512)S(1)}, u32[]{:S(2)}) copy-start(f32[384]{0:T(512)S(1)} %get-tuple-element.231) | copy-start | bytes 4612
  478.6 284.9 %copy-start.27 = (f32[384]{0:T(512)}, f32[384]{0:T(512)S(1)}, u32[]{:S(2)}) copy-start(f32[384]{0:T(512)S(1)} %get-tuple-element.230) | copy-start | bytes 4612
  483.2 35.3 %collective-permute-start = (bf16[384,1024]{1,0:T(8,128)(2,1)S(1)}, bf16[384,1024]{1,0:T(8,128)(2,1)}, u32[]{:S(2)}, u32[]{:S(2)}) collective-permute-start(bf16[384,1024]{1,0:T(8,128)(2,1)S(1)} %get-tuple-element.216), channel_id=1, source_target_pairs={{0,1},{1,2},{2,3},{3,4},{4,5},{5,6},{6,7},{7,0},{8,9},{9,10},{10,1... | collective-permute-start | bytes 2359304 | tf_op jit(solution)/shard_map/ppermute | solution.py:196
  484.7 36.3 %collective-permute-start.1 = (bf16[384,1024]{1,0:T(8,128)(2,1)S(1)}, bf16[384,1024]{1,0:T(8,128)(2,1)}, u32[]{:S(2)}, u32[]{:S(2)}) collective-permute-start(bf16[384,1024]{1,0:T(8,128)(2,1)S(1)} %get-tuple-element.216), channel_id=1, source_target_pairs={{0,7},{1,0},{2,1},{3,2},{4,3},{5,4},{6,5},{7,6},{8,15},{9,8},{10,9... | collective-permute-start | bytes 2359304 | tf_op jit(solution)/shard_map/ppermute | solution.py:201
  518.4 35.8 %collective-permute-start.2 = (bf16[384,1024]{1,0:T(8,128)(2,1)}, bf16[384,1024]{1,0:T(8,128)(2,1)}, u32[]{:S(2)}, u32[]{:S(2)}) collective-permute-start(bf16[384,1024]{1,0:T(8,128)(2,1)} %collective-permute-done), channel_id=1, source_target_pairs={{0,1},{1,2},{2,3},{3,4},{4,5},{5,6},{6,7},{7,0},{8,9},{9,10},{10,1... | collective-permute-start | bytes 2359304 | tf_op jit(solution)/shard_map/ppermute | solution.py:196
  521.0 35.7 %collective-permute-start.3 = (bf16[384,1024]{1,0:T(8,128)(2,1)}, bf16[384,1024]{1,0:T(8,128)(2,1)}, u32[]{:S(2)}, u32[]{:S(2)}) collective-permute-start(bf16[384,1024]{1,0:T(8,128)(2,1)} %collective-permute-done.1), channel_id=1, source_target_pairs={{0,7},{1,0},{2,1},{3,2},{4,3},{5,4},{6,5},{7,6},{8,15},{9,8},{10,9... | collective-permute-start | bytes 2359304 | tf_op jit(solution)/shard_map/ppermute | solution.py:201
  523.2 238.1 %reduce-scatter.16.cloned.1.call-start = ((), (), s32[]{:S(2)}) async-start(), calls=%async_computation.18 | async-start | bytes 7077888 | tf_op jit(solution)/shard_map/reduce_scatter | solution.py:255
  554.3 35.7 %collective-permute-start.4 = (bf16[384,1024]{1,0:T(8,128)(2,1)}, bf16[384,1024]{1,0:T(8,128)(2,1)}, u32[]{:S(2)}, u32[]{:S(2)}) collective-permute-start(bf16[384,1024]{1,0:T(8,128)(2,1)} %collective-permute-done.2), channel_id=1, source_target_pairs={{0,1},{1,2},{2,3},{3,4},{4,5},{5,6},{6,7},{7,0},{8,9},{9,10},{10,1... | collective-permute-start | bytes 2359304 | tf_op jit(solution)/shard_map/ppermute | solution.py:196
  556.7 46.4 %collective-permute-start.5 = (bf16[384,1024]{1,0:T(8,128)(2,1)}, bf16[384,1024]{1,0:T(8,128)(2,1)}, u32[]{:S(2)}, u32[]{:S(2)}) collective-permute-start(bf16[384,1024]{1,0:T(8,128)(2,1)} %collective-permute-done.3), channel_id=1, source_target_pairs={{0,7},{1,0},{2,1},{3,2},{4,3},{5,4},{6,5},{7,6},{8,15},{9,8},{10,9... | collective-permute-start | bytes 2359304 | tf_op jit(solution)/shard_map/ppermute | solution.py:201
  589.9 21.5 %collective-permute-start.6 = (bf16[384,1024]{1,0:T(8,128)(2,1)}, bf16[384,1024]{1,0:T(8,128)(2,1)S(1)}, u32[]{:S(2)}, u32[]{:S(2)}) collective-permute-start(bf16[384,1024]{1,0:T(8,128)(2,1)} %collective-permute-done.4), channel_id=1, source_target_pairs={{0,1},{1,2},{2,3},{3,4},{4,5},{5,6},{6,7},{7,0},{8,9},{9,10},{10,1... | collective-permute-start | bytes 2359304 | tf_op jit(solution)/shard_map/ppermute | solution.py:196
  621.6 13.5 copy-start.35
  635.0 3.5 copy-start.37
  635.0 3.5 copy-start.34
  646.3 218.6 %all-gather.19.cloned.1.call-start = ((), (), s32[]{:S(2)}) async-start(), calls=%async_computation.19 | async-start | bytes 7077888 | tf_op jit(solution)/shard_map/all_gather | solution.py:268
  766.8 363.3 %reduce-scatter.32.cloned.1.call-start = ((), (), s32[]{:S(2)}) async-start(), calls=%async_computation.27 | async-start | bytes 1310720 | tf_op jit(solution)/shard_map/reduce_scatter | solution.py:304
  775.0 357.1 %reduce-scatter.30.cloned.1.call-start = ((), (), s32[]{:S(2)}) async-start(), calls=%async_computation.26 | async-start | bytes 1310720 | tf_op jit(solution)/shard_map/reduce_scatter | solution.py:301
  783.3 350.5 %reduce-scatter.28.cloned.1.call-start = ((), (), s32[]{:S(2)}) async-start(), calls=%async_computation.25 | async-start | bytes 1310720 | tf_op jit(solution)/shard_map/reduce_scatter | solution.py:298
  791.7 344.0 %reduce-scatter.26.cloned.1.call-start = ((), (), s32[]{:S(2)}) async-start(), calls=%async_computation.24 | async-start | bytes 327680 | tf_op jit(solution)/shard_map/reduce_scatter | solution.py:295
  869.7 267.5 %reduce-scatter.20.cloned.1.call-start = ((), (), s32[]{:S(2)}) async-start(), calls=%async_computation.21 | async-start | bytes 327680 | tf_op jit(solution)/shard_map/reduce_scatter | solution.py:286
  881.3 3.0 copy-start.16
  889.1 8.9 copy-start.17
  914.9 3.0 copy-start.16
  922.7 8.9 copy-start.17
  956.3 8.9 copy-start.17
  989.8 8.9 copy-start.17
  1023.3 8.9 copy-start.17
  1056.7 8.9 copy-start.17
  1079.9 6.8 copy-start.13
  1081.2 13.3 slice-start
  1086.7 52.0 %reduce-scatter.22.cloned.1.call-start = ((), (), s32[]{:S(2)}) async-start(), calls=%async_computation.22 | async-start | bytes 327680 | tf_op jit(solution)/shard_map/reduce_scatter | solution.py:289
  1086.7 7.7 slice-start.1
  1086.7 7.7 copy-start.7
  1097.1 6.5 copy-start.18
  1097.1 53.3 %reduce-scatter.24.cloned.1.call-start = ((), (), s32[]{:S(2)}) async-start(), calls=%async_computation.23 | async-start | bytes 327680 | tf_op jit(solution)/shard_map/reduce_scatter | solution.py:292
  1103.5 5.5 copy-start.9
  1109.0 163.1 %reduce-scatter.18.cloned.1.call-start = ((), (), s32[]{:S(2)}) async-start(), calls=%async_computation.20 | async-start | bytes 7077888 | tf_op jit(solution)/shard_map/reduce_scatter | solution.py:311
  1121.3 272.7 %reduce-scatter.14.cloned.1.call-start = ((), (), s32[]{:S(2)}) async-start(), calls=%async_computation.16 | async-start | bytes 7077888 | tf_op jit(solution)/shard_map/reduce_scatter | solution.py:211
  1130.0 142.1 %copy-start.3 = (bf16[384,1024]{1,0:T(8,128)(2,1)S(1)}, bf16[384,1024]{1,0:T(8,128)(2,1)}, u32[]{:S(2)}) copy-start(bf16[384,1024]{1,0:T(8,128)(2,1)} %param.17) | copy-start | bytes 2359300
  1130.0 142.1 %copy-start.22 = (f32[4,1,256]{2,1,0:T(1,128)S(1)}, f32[4,1,256]{2,1,0:T(1,128)}, u32[]{:S(2)}) copy-start(f32[4,1,256]{2,1,0:T(1,128)} %copy-done.21) | copy-start | bytes 12292
  1130.0 142.1 %copy-start.26 = (f32[384]{0:T(512)S(1)}, f32[384]{0:T(512)}, u32[]{:S(2)}) copy-start(f32[384]{0:T(512)} %copy-done.25) | copy-start | bytes 4612
  1130.0 143.7 %copy-start.31 = (f32[1024]{0:T(1024)S(1)}, f32[1024]{0:T(1024)}, u32[]{:S(2)}) copy-start(f32[1024]{0:T(1024)} %get-tuple-element.167) | copy-start | bytes 12292
  1130.0 264.0 %copy-start.2 = (f32[384,1024]{1,0:T(8,128)S(1)}, f32[384,1024]{1,0:T(8,128)}, u32[]{:S(2)}) copy-start(f32[384,1024]{1,0:T(8,128)} %copy-done.1) | copy-start | bytes 4718596
  1130.0 264.0 %copy-start.6 = (bf16[384,1024]{1,0:T(8,128)(2,1)S(1)}, bf16[384,1024]{1,0:T(8,128)(2,1)}, u32[]{:S(2)}) copy-start(bf16[384,1024]{1,0:T(8,128)(2,1)} %param.29) | copy-start | bytes 2359300
  1130.0 263.9 %copy-start.20 = (f32[4,1,256]{2,1,0:T(1,128)S(1)}, f32[4,1,256]{2,1,0:T(1,128)}, u32[]{:S(2)}) copy-start(f32[4,1,256]{2,1,0:T(1,128)} %copy-done.19) | copy-start | bytes 12292
  1130.0 263.9 %copy-start.24 = (f32[384]{0:T(512)S(1)}, f32[384]{0:T(512)}, u32[]{:S(2)}) copy-start(f32[384]{0:T(512)} %copy-done.23) | copy-start | bytes 4612
  1130.0 263.9 %copy-start.28 = (f32[384]{0:T(512)S(1)}, f32[384]{0:T(512)}, u32[]{:S(2)}) copy-start(f32[384]{0:T(512)} %copy-done.27) | copy-start | bytes 4612
  1130.1 263.9 %copy-start.30 = (f32[384]{0:T(512)S(1)}, f32[384]{0:T(512)}, u32[]{:S(2)}) copy-start(f32[384]{0:T(512)} %copy-done.29) | copy-start | bytes 4612
  1130.1 263.9 %copy-start.32 = (f32[384]{0:T(512)S(1)}, f32[384]{0:T(512)}, u32[]{:S(2)}) copy-start(f32[384]{0:T(512)} %get-tuple-element.228) | copy-start | bytes 4612
  (10 other events, 22.9 us)
Sparse Core Ops, SparseCore 0:
  19.1 100.8 all-gather.8
  225.9 250.7 reduce-scatter.11
Sparse Core Ops, SparseCore 1:
  227.8 14.9 all-gather.14
  244.8 168.4 all-gather.16
  414.6 15.6 all-gather.12
  523.3 14.1 all-gather.10
  646.4 114.8 reduce-scatter.15
  766.9 98.0 all-gather.18
  867.3 22.9 reduce-scatter.31
  892.9 24.8 reduce-scatter.29
  920.1 24.8 reduce-scatter.27
  947.6 19.9 reduce-scatter.25
  1086.7 18.0 reduce-scatter.19
  1108.0 19.9 reduce-scatter.21
  1130.3 20.0 reduce-scatter.23
  1154.4 117.6 reduce-scatter.17
  1276.1 117.8 reduce-scatter.13
